TPU v7x, 1024 devices: a whole 8x8x8 slice. The times are simulated.
1024 devices in a mesh: blk: 16 (over z_lo, y), grp: 64 (over x, z_hi, core).
Axes of the slice: x: 8, y: 8, z: 8 (z_hi: 4, z_lo: 2; z = z_hi * 2 + z_lo), core: 2. Of those that a mesh axis runs over, the one named last changes fastest.
Arguments:
- queries: bfloat16 [32, 128, 1280], P('blk'), may hold values from -8 to 8
- query_lengths: int32 [32], P('blk'), may hold values from 32 to 128, as said below
- targets: bfloat16 [4096, 128, 1280], P(('blk', 'grp')), may hold values from -8 to 8
- target_lengths: int32 [4096], P(('blk', 'grp')), may hold values from 32 to 128, as said below
Outputs:
- profile: float32 [32, 128, 1280], P('blk', 'grp')
- similarity: float32 [32, 1024], P('blk', 'grp')
Inputs may be any that keep to these rules, and one draw needn't show every extreme that they name: The first query_lengths[q] residues of query q are valid, the rest is padding; some query has all 128. The first target_lengths[t] residues of target t are valid, the rest is padding; some target has all 128.
All inputs are finite; a program needn't handle non-finite values.
Results may differ from a plain program's by a relative error of at most 0.00079.
Values may be sent and summed in bfloat16 or wider, within the bound.
No kernel may reach another device: no remote copies, remote signals or barrier semaphores. Data moves between devices by JAX's collectives and lax.ppermute only.
A program may use at most 32 MiB of HBM per device.

v0:
```python
import math

import jax
import jax.numpy as jnp
from jax import lax
from jax.sharding import PartitionSpec as P

STEPS = 3


def for_sending(array):

    def short(part):
        return part.astype(jnp.bfloat16) if part.dtype == jnp.float32 else part

    return jax.tree.map(short, array)


def from_behind(array, axis, by):
    length = lax.axis_size(axis)
    return lax.ppermute(array, axis, [(i, (i + by) % length) for i in range(length)])


def align_pair(query_rows, query_len, target_rows, target_len):
    scale = 3.0 / math.sqrt(query_rows.shape[-1])
    scores = (
        jnp.einsum("qid,mjd->qmij", query_rows, target_rows, preferred_element_type=jnp.float32)
        * scale
    )
    positions = lax.broadcasted_iota(jnp.float32, (1, query_rows.shape[1]), 1)
    row_ok = positions < query_len[:, None]
    col_ok = positions < target_len[:, None]
    row_mask = row_ok[:, None, :, None]
    col_mask = col_ok[None, :, None, :]
    row_top = jnp.max(jnp.where(col_mask, scores, -jnp.inf), axis=3, keepdims=True)
    row_exp = jnp.where(col_mask, jnp.exp(scores - row_top), 0.0)
    row_soft = jnp.where(row_mask, row_exp / jnp.sum(row_exp, axis=3, keepdims=True), 0.0)
    col_top = jnp.max(jnp.where(row_mask, scores, -jnp.inf), axis=2, keepdims=True)
    col_exp = jnp.where(row_mask, jnp.exp(scores - col_top), 0.0)
    col_soft = jnp.where(col_mask, col_exp / jnp.sum(col_exp, axis=2, keepdims=True), 0.0)
    weights = row_soft + col_soft - row_soft * col_soft
    similarity = jnp.sum(weights * scores, axis=(2, 3)) / jnp.sum(weights, axis=(2, 3))
    profile = jnp.einsum(
        "qmij,mjd->qid",
        row_soft.astype(jnp.bfloat16),
        target_rows,
        preferred_element_type=jnp.float32,
    )
    return (similarity, profile)


def shards(queries, query_lengths, targets, target_lengths):
    blocks = targets.shape[0]
    group_size = lax.axis_size("grp")
    profile_scale = 1.0 / math.sqrt(group_size * blocks * (STEPS + 1))
    resident = (targets, target_lengths.astype(jnp.bfloat16))
    running = jnp.zeros(queries.shape, jnp.float32)
    arrived = [resident]
    for offset in range(STEPS):
        arrived.append(from_behind(for_sending(arrived[-1]), "blk", 1))
    query_len = query_lengths.astype(jnp.float32)
    collected = []
    for visiting in arrived:
        pair_sim, pair_prof = align_pair(
            queries, query_len, visiting[0], visiting[1].astype(jnp.float32)
        )
        running = running + pair_prof
        collected.append(pair_sim)
    similarity = jnp.concatenate(collected, axis=1)
    shares = lax.psum_scatter(running, "grp", scatter_dimension=1, tiled=True) * profile_scale
    return (shares, similarity)


def solution(mesh):
    in_specs = (P("blk", None, None), P("blk"), P(("blk", "grp"), None, None), P(("blk", "grp")))
    out_specs = (P("blk", "grp", None), P("blk", "grp"))
    return jax.shard_map(shards, mesh=mesh, in_specs=in_specs, out_specs=out_specs, check_vma=False)
```

profile of v0, /device:TPU:1, one launch (start us, length us, event | category | flops | bytes accessed | tf_op | source)
XLA Modules:
  0.0 697.8 jit_solution(11860269566335344668)
XLA Ops:
  7.2 4.3 collective-permute-start.1
  12.2 3.3 collective-permute-start
  16.2 2.0 fusion.38
  18.8 16.9 %collective-permute-done.1 = bf16[4,128,1280]{2,1,0:T(8,128)(2,1)S(1)} collective-permute-done((bf16[4,128,1280]{2,1,0:T(8,128)(2,1)}, bf16[4,128,1280]{2,1,0:T(8,128)(2,1)S(1)}, u32[]{:S(2)}, u32[]{:S(2)}) %collective-permute-start.1) | collective-permute-done | bytes 1310752 | tf_op jit(solution)/shard_map/ppermute | solution.py:21
  35.7 6.9 collective-permute-start.3
  43.2 4.0 collective-permute-start.2
  47.3 26.5 %collective-permute-done.2 = bf16[4]{0:T(256)(128)(2,1)S(1)} collective-permute-done((bf16[4]{0:T(256)(128)(2,1)S(1)}, bf16[4]{0:T(256)(128)(2,1)S(1)}, u32[]{:S(2)}, u32[]{:S(2)}) %collective-permute-start.2) | collective-permute-done | bytes 40 | tf_op jit(solution)/shard_map/ppermute | solution.py:21
  73.9 1.9 collective-permute-start.4
  75.9 4.4 collective-permute-done.4
  80.9 1.9 collective-permute-start.5
  82.9 1.0 fusion.171
  83.9 3.2 fusion.14
  87.1 1.9 fusion.50
  90.1 3.6 fusion.13
  93.6 16.3 %collective-permute-done.5 = bf16[4,128,1280]{2,1,0:T(8,128)(2,1)} collective-permute-done((bf16[4,128,1280]{2,1,0:T(8,128)(2,1)}, bf16[4,128,1280]{2,1,0:T(8,128)(2,1)}, u32[]{:S(2)}, u32[]{:S(2)}) %collective-permute-start.5) | collective-permute-done | bytes 1310752 | tf_op jit(solution)/shard_map/ppermute | solution.py:21
  110.0 1.9 fusion.56
  112.4 3.6 fusion.12
  116.7 1.1 fusion.165
  117.9 1.3 dynamic-slice
  119.8 2.2 fusion.166
  122.2 2.7 fusion.167
  125.0 1.1 fusion.168
  126.9 562.6 %all-reduce.3.cloned.1.call-done = f32[2,128,1280]{2,1,0:T(8,128)} async-done(((f32[2,128,1280]{2,1,0:T(8,128)}), f32[2,128,1280]{2,1,0:T(8,128)}) %all-reduce.3.cloned.1.call-update) | async-done | bytes 1310736
  689.5 1.5 dynamic-slice_multiply_fusion
  (50 shorter events, 6.8 us)
Async XLA Ops:
  7.2 9.0 %copy-start = (bf16[2,128,1280]{2,1,0:T(8,128)(2,1)S(1)}, bf16[2,128,1280]{2,1,0:T(8,128)(2,1)}, u32[]{:S(2)}) copy-start(bf16[2,128,1280]{2,1,0:T(8,128)(2,1)} %param.4) | copy-start | bytes 1966084
  7.2 682.3 %all-reduce.3.cloned.1.call-start = ((), (), s32[]{:S(2)}) async-start(), calls=%async_computation | async-start | bytes 2621440
  7.2 28.5 %collective-permute-start.1 = (bf16[4,128,1280]{2,1,0:T(8,128)(2,1)}, bf16[4,128,1280]{2,1,0:T(8,128)(2,1)S(1)}, u32[]{:S(2)}, u32[]{:S(2)}) collective-permute-start(bf16[4,128,1280]{2,1,0:T(8,128)(2,1)} %param.6), channel_id=1, source_target_pairs={{0,64},{64,128},{128,192},{192,256},{256,320},{320,384},{384,448},... | collective-permute-start | bytes 3932168 | tf_op jit(solution)/shard_map/ppermute | solution.py:21
  12.2 31.1 %collective-permute-start = (bf16[4]{0:T(256)(128)(2,1)S(1)}, bf16[4]{0:T(256)(128)(2,1)S(1)}, u32[]{:S(2)}, u32[]{:S(2)}) collective-permute-start(bf16[4]{0:T(256)(128)(2,1)S(1)} %get-tuple-element.12), channel_id=1, source_target_pairs={{0,64},{64,128},{128,192},{192,256},{256,320},{320,384},{384,448},... | collective-permute-start | bytes 32 | tf_op jit(solution)/shard_map/ppermute | solution.py:21
  16.2 2.0 copy-start.4
  16.2 26.5 %copy-start.1 = (bf16[4,128,1280]{2,1,0:T(8,128)(2,1)S(1)}, bf16[4,128,1280]{2,1,0:T(8,128)(2,1)}, u32[]{:S(2)}) copy-start(bf16[4,128,1280]{2,1,0:T(8,128)(2,1)} %param.6) | copy-start | bytes 3932164
  35.7 44.7 %copy-start.10 = (bf16[4,128,1280]{2,1,0:T(8,128)(2,1)}, bf16[4,128,1280]{2,1,0:T(8,128)(2,1)S(1)}, u32[]{:S(2)}) copy-start(bf16[4,128,1280]{2,1,0:T(8,128)(2,1)S(1)} %collective-permute-done.1) | copy-start | bytes 3932164
  35.7 45.2 %collective-permute-start.3 = (bf16[4,128,1280]{2,1,0:T(8,128)(2,1)S(1)}, bf16[4,128,1280]{2,1,0:T(8,128)(2,1)}, u32[]{:S(2)}, u32[]{:S(2)}) collective-permute-start(bf16[4,128,1280]{2,1,0:T(8,128)(2,1)S(1)} %collective-permute-done.1), channel_id=1, source_target_pairs={{0,64},{64,128},{128,192},{192,256},{256,320},{320,384},{384,448},... | collective-permute-start | bytes 3932168 | tf_op jit(solution)/shard_map/ppermute | solution.py:21
  42.7 37.6 %copy-start.8 = (pred[2,128]{1,0:T(4,128)(4,1)}, pred[2,128]{1,0:T(4,128)(4,1)S(1)}, u32[]{:S(2)}) copy-start(pred[2,128]{1,0:T(4,128)(4,1)S(1)} %iota_compare_fusion.4) | copy-start | bytes 772
  43.2 30.6 %collective-permute-start.2 = (bf16[4]{0:T(256)(128)(2,1)S(1)}, bf16[4]{0:T(256)(128)(2,1)S(1)}, u32[]{:S(2)}, u32[]{:S(2)}) collective-permute-start(bf16[4]{0:T(256)(128)(2,1)S(1)} %collective-permute-done), channel_id=1, source_target_pairs={{0,64},{64,128},{128,192},{192,256},{256,320},{320,384},{384,448},... | collective-permute-start | bytes 32 | tf_op jit(solution)/shard_map/ppermute | solution.py:21
  47.3 35.5 %copy-start.6 = (pred[4,128]{1,0:T(4,128)(4,1)}, pred[4,128]{1,0:T(4,128)(4,1)S(1)}, u32[]{:S(2)}) copy-start(pred[4,128]{1,0:T(4,128)(4,1)S(1)} %iota_compare_fusion.2) | copy-start | bytes 1540
  73.9 6.4 collective-permute-start.4
  80.9 29.0 %collective-permute-start.5 = (bf16[4,128,1280]{2,1,0:T(8,128)(2,1)}, bf16[4,128,1280]{2,1,0:T(8,128)(2,1)}, u32[]{:S(2)}, u32[]{:S(2)}) collective-permute-start(bf16[4,128,1280]{2,1,0:T(8,128)(2,1)} %collective-permute-done.3), channel_id=1, source_target_pairs={{0,64},{64,128},{128,192},{192,256},{256,320},{320,384},{384,448},... | collective-permute-start | bytes 3932168 | tf_op jit(solution)/shard_map/ppermute | solution.py:21
  87.1 2.9 copy-start.9
  89.0 4.6 copy-start.2
  116.0 0.7 copy-start.5
  116.6 3.2 copy-start.7
  119.8 2.3 copy-start.3
Sparse Core Ops, SparseCore 0:
  116.1 573.2 all-reduce.2
where the time goes:
time: 698 us
  waiting for transfers between devices  627 us (90%)
  starting transfers between devices  22.3 us (3%)
  matrix products  17.1 us (2%)
  between operations  14.9 us (2%)
  other arithmetic  14.3 us (2%)
    unnamed x2, waiting for transfers between devices  563 us
    ppermute x6, waiting for transfers between devices, from_behind(): lax.ppermute(array, axis, [(i, (i + by) % length) for i in range(length)])  64.2 us
    ppermute x6, starting transfers between devices, from_behind(): lax.ppermute(array, axis, [(i, (i + by) % length) for i in range(length)])  22.3 us
  transfers between devices with their start and end apart: 7, of which 5 were waited for; matrix products, arithmetic and copies ran while one was open for 4% of the time, Pallas kernels for 0%

commit v1 on v0

v1 whole, which is shorter than its diff:
```python
import math

import jax
import jax.numpy as jnp
from jax import lax
from jax.experimental import pallas as pl
from jax.experimental.pallas import tpu as pltpu
from jax.sharding import Mesh
from jax.sharding import PartitionSpec as P

BLK = ("zl", "y")
GRP = ("x", "zh", "core")
STEPS = 3
NX, NZ = 8, 4
F32 = jnp.float32
BF16 = jnp.bfloat16


def soft_block(q_ref, t_ref, qlen_ref, tlen_ref, offset, sims):
    queries, length, width = q_ref.shape
    blocks = t_ref.shape[0]
    scale = 3.0 / math.sqrt(width)
    scores = (
        lax.dot_general(
            q_ref[...].reshape(queries * length, width),
            t_ref[...].reshape(blocks * length, width),
            (((1,), (1,)), ((), ())),
            preferred_element_type=F32,
        )
        * scale
    )
    lanes = lax.broadcasted_iota(jnp.int32, (length, length), 1)
    rows = lax.broadcasted_iota(jnp.int32, (length, length), 0)
    place_row = lax.broadcasted_iota(jnp.int32, sims.shape, 0)
    place_lane = lax.broadcasted_iota(jnp.int32, sims.shape, 1)
    stacked = []
    for q in range(queries):
        row_ok = rows < qlen_ref[q]
        row_on = lax.broadcasted_iota(jnp.int32, (length, 1), 0) < qlen_ref[q]
        pieces = []
        for m in range(blocks):
            col_ok = lanes < tlen_ref[m]
            col_on = lax.broadcasted_iota(jnp.int32, (1, length), 1) < tlen_ref[m]
            s = scores[q * length : (q + 1) * length, m * length : (m + 1) * length]
            by_row = jnp.where(col_ok, s, -jnp.inf)
            row_exp = jnp.exp(by_row - jnp.max(by_row, axis=1, keepdims=True))
            row_soft = row_exp * jnp.where(row_on, 1.0 / jnp.sum(row_exp, axis=1, keepdims=True), 0.0)
            by_col = jnp.where(row_ok, s, -jnp.inf)
            col_exp = jnp.exp(by_col - jnp.max(by_col, axis=0, keepdims=True))
            col_soft = col_exp * jnp.where(col_on, 1.0 / jnp.sum(col_exp, axis=0, keepdims=True), 0.0)
            weights = row_soft + col_soft - row_soft * col_soft
            over = jnp.sum(jnp.sum(weights * s, axis=0, keepdims=True), axis=1, keepdims=True)
            under = jnp.sum(jnp.sum(weights, axis=0, keepdims=True), axis=1, keepdims=True)
            here = jnp.logical_and(place_row == q, place_lane == offset * blocks + m)
            sims = jnp.where(here, over / under, sims)
            pieces.append(row_soft.astype(BF16))
        stacked.append(jnp.concatenate(pieces, axis=1))
    return jnp.concatenate(stacked, axis=0), sims


def ordered(align, core_ref):
    total = align.shape[0]
    p = lax.broadcasted_iota(jnp.int32, (total, total), 0)
    i = lax.broadcasted_iota(jnp.int32, (total, total), 1)
    core = jnp.bitwise_xor(p >> 8, core_ref[0])
    source = ((p >> 1) & 3) * 128 + ((p >> 3) & 31) * 4 + core * 2 + (p & 1)
    pick = jnp.where(i == source, 1.0, 0.0).astype(BF16)
    return jnp.dot(pick, align, preferred_element_type=F32).astype(BF16)


def own_kernel(qlen_ref, tlen_ref, q_ref, t_ref, align_ref, sims_ref):
    align, sims = soft_block(q_ref, t_ref, qlen_ref, tlen_ref, 0, jnp.zeros(sims_ref.shape, F32))
    align_ref[...] = align
    sims_ref[...] = sims


def rest_kernel(
    core_ref, qlen_ref, qlen2_ref, tlen_ref, tlen1_ref, q_ref, q2_ref, t_ref, t1_ref, align_ref, sims_ref,
    mine_ref, theirs_ref, sims01_ref, sims23_ref, every_ref,
):
    flat = (t_ref.shape[0] * t_ref.shape[1], t_ref.shape[2])
    rows, columns = align_ref.shape
    every_ref[:rows, :columns] = align_ref[...]
    every_ref[rows:, :columns], sims = soft_block(q2_ref, t_ref, qlen2_ref, tlen_ref, 2, jnp.zeros(sims_ref.shape, F32))
    every_ref[:rows, columns:], sims01_ref[...] = soft_block(q_ref, t1_ref, qlen_ref, tlen1_ref, 1, sims_ref[...])
    every_ref[rows:, columns:], sims23_ref[...] = soft_block(q2_ref, t1_ref, qlen2_ref, tlen1_ref, 3, sims)
    align = ordered(every_ref[...], core_ref)
    partial = jnp.dot(align[:, :columns], t_ref[...].reshape(flat), preferred_element_type=F32)
    partial += jnp.dot(align[:, columns:], t1_ref[...].reshape(flat), preferred_element_type=F32)
    mine_ref[...] = partial[:rows].reshape(mine_ref.shape)
    theirs_ref[...] = partial[rows:].reshape(theirs_ref.shape)


def pack_kernel(mine_ref, theirs_ref, packed_ref, total_ref):
    total_ref[...] = mine_ref[...] + theirs_ref[...]
    top = jnp.max(jnp.abs(total_ref[...]), axis=0)
    top = jnp.max(jnp.max(top, axis=0, keepdims=True), axis=1, keepdims=True)
    power = jnp.floor(14.5 - jnp.log(jnp.maximum(top, 1e-30)) * (1.0 / math.log(2.0)))
    width = mine_ref.shape[2]
    packed_ref[:, :, :width] = total_ref[...] * jnp.exp2(power)[None]
    side = (mine_ref.shape[0], mine_ref.shape[1], packed_ref.shape[2] - width)
    packed_ref[:, :, width:] = jnp.broadcast_to(power[None], side)


def unpacked_sum(packed_ref, width):
    total = jnp.zeros((packed_ref.shape[1], width), F32)
    for n in range(packed_ref.shape[0]):
        total += packed_ref[n, :, :width] * jnp.exp2(-packed_ref[n, :, width : width + 1])
    return total


def hand_on(total, sims_ref, own_ref, message_ref):
    half = own_ref.shape[0]
    own_ref[...] = total[:half]
    message_ref[...] = jnp.zeros(message_ref.shape, F32)
    message_ref[0:half, :] = total[half:]
    message_ref[half : half + 2, 0 : sims_ref.shape[1]] = sims_ref[0:2, :]


def sum_kernel(packed_ref, total_ref):
    total_ref[...] = unpacked_sum(packed_ref, total_ref.shape[1])


def tail_kernel(pieces_ref, sims_ref, own_ref, message_ref):
    hand_on(jnp.sum(pieces_ref[...], axis=0), sims_ref, own_ref, message_ref)


def packed_tail_kernel(packed_ref, sims_ref, own_ref, message_ref):
    hand_on(unpacked_sum(packed_ref, own_ref.shape[1]), sims_ref, own_ref, message_ref)


SMEM = pl.BlockSpec(memory_space=pltpu.SMEM)
VMEM = pl.BlockSpec(memory_space=pltpu.VMEM)


def call(kernel, scalars, arrays, outs, flops, name, scratch=()):
    moved = sum(a.size * a.dtype.itemsize for a in [*arrays, *outs])
    return pl.pallas_call(
        kernel,
        out_shape=outs,
        in_specs=[SMEM] * len(scalars) + [VMEM] * len(arrays),
        out_specs=[VMEM] * len(outs),
        scratch_shapes=list(scratch),
        cost_estimate=pl.CostEstimate(flops=flops, bytes_accessed=moved, transcendentals=0),
        compiler_params=pltpu.CompilerParams(vmem_limit_bytes=20 << 20),
        name=name,
    )(*scalars, *arrays)


def moved_by(array, by):
    length = lax.axis_size(BLK)
    return lax.ppermute(array, BLK, [(i, (i + by) % length) for i in range(length)])


def shards(queries, query_lengths, targets, target_lengths):
    count, length, width = queries.shape
    blocks = targets.shape[0]
    profile_scale = 1.0 / math.sqrt(lax.axis_size(GRP) * blocks * (STEPS + 1))
    core = lax.axis_index("core").reshape(1)
    struct = jax.ShapeDtypeStruct
    pair_flops = 2 * count * blocks * length * length * width

    targets1 = moved_by(targets, 1)
    queries2 = moved_by(queries, -2)
    lengths1 = moved_by(target_lengths, 1)
    query_lengths2 = moved_by(query_lengths, -2)

    sims_shape = struct((8, 128), F32)
    rows = count * length
    align, sims = call(
        own_kernel, [query_lengths, target_lengths], [queries, targets],
        [struct((rows, blocks * length), BF16), sims_shape], pair_flops, "own_pairs",
    )
    owned = rows // (NX * NZ)
    halves = struct((NX * NZ, owned, width), F32)
    mine, theirs, sims01, sims23 = call(
        rest_kernel, [core, query_lengths, query_lengths2, target_lengths, lengths1],
        [queries, queries2, targets, targets1, align, sims],
        [halves, halves, sims_shape, sims_shape], 8 * pair_flops, "other_pairs",
        [pltpu.VMEM((2 * rows, 2 * blocks * length), BF16)],
    )

    theirs = lax.ppermute(theirs, "core", [(0, 1), (1, 0)])
    packed_shape = struct((NX * NZ, owned, width + 128), F32)
    (packed,) = call(
        pack_kernel, [], [mine, theirs], [packed_shape], 8 * mine.size, "pack", [pltpu.VMEM(mine.shape, F32)]
    )
    half = owned // 2
    ends = [struct((half, width), F32), struct((owned, width), F32)]
    packed = lax.all_to_all(packed.astype(jnp.float16), ("x", "zh"), 0, 0, tiled=True).astype(F32)
    own, message = call(packed_tail_kernel, [], [packed, sims23], ends, packed.size, "tail")
    message = moved_by(message, 2)
    profile = (own + message[:half]) * profile_scale
    columns = blocks * (STEPS + 1)
    similarity = sims01[:count, :columns] + message[half : half + count, :columns]
    return (profile.reshape(count, half // count, width), similarity)


def solution(mesh):
    cut = Mesh(mesh.devices.reshape(2, 8, NX, NZ, 2), BLK + GRP)
    in_specs = (P(BLK, None, None), P(BLK), P(BLK + GRP, None, None), P(BLK + GRP))
    out_specs = (P(BLK, GRP, None), P(BLK, GRP))
    return jax.shard_map(shards, mesh=cut, in_specs=in_specs, out_specs=out_specs, check_vma=False)
```

time: 698 us -> 106 us (0.15)
  the two profiles are of different devices: /device:TPU:1 before, /device:TPU:2 now
where the time goes in v1:
time: 106 us
  blocking collectives  43.5 us (41%)
  waiting for transfers between devices  25.4 us (24%)
  starting transfers between devices  23.9 us (23%)
  Pallas kernels  6.98 us (7%)
  local copies, waits for them, and re-layouts  4.34 us (4%)
    all_to_all x1, blocking collectives, shards(): lax.all_to_all(packed.astype(jnp.float16), ('x', 'zh'), 0, 0, tiled=True)  43.5 us
    ppermute x5, waiting for transfers between devices, moved_by(): lax.ppermute(array, BLK, [(i, (i + by) % length) for i in range(length)])  22.4 us
    ppermute x5, starting transfers between devices, moved_by(): lax.ppermute(array, BLK, [(i, (i + by) % length) for i in range(length)])  21.9 us
    pallas_call x4, Pallas kernels, call(): pl.pallas_call(kernel, out_shape=outs, in_specs=[SMEM] * len(scalars) + [...  6.98 us
    unnamed x8, local copies, waits for them, and re-layouts  3.71 us
    ppermute x1, waiting for transfers between devices, shards(): theirs = lax.ppermute(theirs, 'core', [(0, 1), (1, 0)])  3 us
  transfers between devices with their start and end apart: 6, of which 3 were waited for; matrix products, arithmetic and copies ran while one was open for 0% of the time, Pallas kernels for 2%

profile of v1, /device:TPU:2, one launch (start us, length us, event | category | flops | bytes accessed | tf_op | source)
XLA Modules:
  0.0 105.6 jit_solution(5196184428819248679)
XLA Ops:
  0.6 3.6 %collective-permute-start.3 = (bf16[4,128,1280]{2,1,0:T(8,128)(2,1)}, bf16[4,128,1280]{2,1,0:T(8,128)(2,1)S(1)}, u32[]{:S(2)}, u32[]{:S(2)}) collective-permute-start(bf16[4,128,1280]{2,1,0:T(8,128)(2,1)} %t_ref.3), channel_id=1, source_target_pairs={{0,64},{64,128},{128,192},{192,256},{256,320},{320,384},{384,448},... | collective-permute-start | bytes 3932168 | tf_op jit(solution)/shard_map/ppermute | solution.py:152
  4.2 8.7 %collective-permute-start.2 = (bf16[2,128,1280]{2,1,0:T(8,128)(2,1)}, bf16[2,128,1280]{2,1,0:T(8,128)(2,1)S(1)}, u32[]{:S(2)}, u32[]{:S(2)}) collective-permute-start(bf16[2,128,1280]{2,1,0:T(8,128)(2,1)} %q_ref.3), channel_id=1, source_target_pairs={{0,896},{64,960},{128,0},{192,64},{256,128},{320,192},{384,256},{4... | collective-permute-start | bytes 1966088 | tf_op jit(solution)/shard_map/ppermute | solution.py:152
  12.9 3.8 %collective-permute-start = (s32[2]{0:T(128)}, s32[2]{0:T(128)S(1)}, u32[]{:S(2)}, u32[]{:S(2)}) collective-permute-start(s32[2]{0:T(128)} %qlen_ref.3), channel_id=1, source_target_pairs={{0,896},{64,960},{128,0},{192,64},{256,128},{320,192},{384,256},{4... | collective-permute-start | bytes 32 | tf_op jit(solution)/shard_map/ppermute | solution.py:152
  16.7 2.7 %collective-permute-start.1 = (s32[4]{0:T(128)}, s32[4]{0:T(128)S(1)}, u32[]{:S(2)}, u32[]{:S(2)}) collective-permute-start(s32[4]{0:T(128)} %tlen_ref.3), channel_id=1, source_target_pairs={{0,64},{64,128},{128,192},{192,256},{256,320},{320,384},{384,448},... | collective-permute-start | bytes 56 | tf_op jit(solution)/shard_map/ppermute | solution.py:152
  19.4 1.3 %copy-done = bf16[4,128,1280]{2,1,0:T(8,128)(2,1)S(1)} copy-done((bf16[4,128,1280]{2,1,0:T(8,128)(2,1)S(1)}, bf16[4,128,1280]{2,1,0:T(8,128)(2,1)}, u32[]{:S(2)}) %copy-start) | copy-done | bytes 1310744
  20.8 1.1 %copy-done.1 = bf16[2,128,1280]{2,1,0:T(8,128)(2,1)S(1)} copy-done((bf16[2,128,1280]{2,1,0:T(8,128)(2,1)S(1)}, bf16[2,128,1280]{2,1,0:T(8,128)(2,1)}, u32[]{:S(2)}) %copy-start.1) | copy-done | bytes 655384
  21.8 0.7 copy-done.2
  22.5 0.7 copy-done.3
  23.2 1.6 %own_pairs.1 = (bf16[256,512]{1,0:T(8,128)(2,1)S(1)}, f32[8,128]{1,0:T(8,128)S(1)}) custom-call(s32[2]{0:T(128)S(1)} %copy-done.2, s32[4]{0:T(128)S(1)} %copy-done.3, bf16[2,128,1280]{2,1,0:T(8,128)(2,1)S(1)} %copy-done.1, bf16[4,128,1280]{2,1,0:T(8,128)(2,1)S(1)} %copy-done), custom_call_target="tpu_custom_call" | custom-call | flops 335544320 | bytes 2232320 | tf_op jit(solution)/shard_map/own_pairs/pallas_call | solution.py:138
  24.8 16.2 %collective-permute-done.qlen2_ref = s32[2]{0:T(128)S(1)} collective-permute-done((s32[2]{0:T(128)}, s32[2]{0:T(128)S(1)}, u32[]{:S(2)}, u32[]{:S(2)}) %collective-permute-start) | collective-permute-done | bytes 40 | tf_op jit(solution)/shard_map/ppermute | solution.py:152
  41.0 0.0 collective-permute-done.1.tlen1_ref
  41.0 0.0 collective-permute-done.2.q2_ref
  41.0 4.9 %other_pairs.1 = (f32[32,8,1280]{2,1,0:T(8,128)S(1)}, f32[32,8,1280]{2,1,0:T(8,128)S(1)}, f32[8,128]{1,0:T(8,128)S(1)}, f32[8,128]{1,0:T(8,128)S(1)}) custom-call(s32[1]{0:T(128)} %bitcast.core_ref, s32[2]{0:T(128)S(1)} %copy-done.2, s32[2]{0:T(128)S(1)} %collective-permute-done.qlen2_ref, s32[4]{0:T(128)S(1)} %copy-done.3, ...), custom_call_target="tpu_custom_call" | custom-call | flops 2684354560 | bytes 6828032 | tf_op jit(solution)/shard_map/other_pairs/pallas_call | solution.py:138
  45.8 1.9 %collective-permute-start.4 = (f32[32,8,1280]{2,1,0:T(8,128)S(1)}, f32[32,8,1280]{2,1,0:T(8,128)S(1)}, u32[]{:S(2)}, u32[]{:S(2)}) collective-permute-start(f32[32,8,1280]{2,1,0:T(8,128)S(1)} %get-tuple-element.13), channel_id=1, source_target_pairs={{0,1},{1,0},{2,3},{3,2},{4,5},{5,4},{6,7},{7,6},{8,9},{9,8},{10,11... | collective-permute-start | bytes 3932168 | tf_op jit(solution)/shard_map/ppermute | solution.py:183
  47.8 3.0 %collective-permute-done.4.theirs_ref = f32[32,8,1280]{2,1,0:T(8,128)S(1)} collective-permute-done((f32[32,8,1280]{2,1,0:T(8,128)S(1)}, f32[32,8,1280]{2,1,0:T(8,128)S(1)}, u32[]{:S(2)}, u32[]{:S(2)}) %collective-permute-start.4) | collective-permute-done | bytes 1310752 | tf_op jit(solution)/shard_map/ppermute | solution.py:183
  50.8 0.4 pack.1
  51.1 0.1 convert_element_type.6
  51.2 43.5 %all_to_all.5 = f16[32,8,1408]{2,1,0:T(8,128)(2,1)S(1)} all-to-all(f16[32,8,1408]{2,1,0:T(8,128)(2,1)S(1)} %convert_element_type.6), channel_id=1, replica_groups=mesh['zl'=2,'y'=8,'x'=8,'zh'=4,'core'=2] {'x','zh'}, dimensions={0} | all-to-all | bytes 1441792 | tf_op jit(solution)/shard_map/all_to_all | solution.py:190
  94.8 0.1 convert_element_type.7.packed_ref
  94.9 0.2 tail.1
  95.0 3.2 %collective-permute-start.5 = (f32[8,1280]{1,0:T(8,128)S(1)}, f32[8,1280]{1,0:T(8,128)S(1)}, u32[]{:S(2)}, u32[]{:S(2)}) collective-permute-start(f32[8,1280]{1,0:T(8,128)S(1)} %get-tuple-element.16), channel_id=1, source_target_pairs={{0,128},{64,192},{128,256},{192,320},{256,384},{320,448},{384,512}... | collective-permute-start | bytes 122888 | tf_op jit(solution)/shard_map/ppermute | solution.py:152
  98.2 6.2 %collective-permute-done.5 = f32[8,1280]{1,0:T(8,128)S(1)} collective-permute-done((f32[8,1280]{1,0:T(8,128)S(1)}, f32[8,1280]{1,0:T(8,128)S(1)}, u32[]{:S(2)}, u32[]{:S(2)}) %collective-permute-start.5) | collective-permute-done | bytes 40992 | tf_op jit(solution)/shard_map/ppermute | solution.py:152
  104.4 0.6 reshape.11
  105.0 0.6 slice_add_fusion.1
  (6 shorter events, 0.0 us)
Async XLA Ops:
  0.6 40.3 %collective-permute-start.3 = (bf16[4,128,1280]{2,1,0:T(8,128)(2,1)}, bf16[4,128,1280]{2,1,0:T(8,128)(2,1)S(1)}, u32[]{:S(2)}, u32[]{:S(2)}) collective-permute-start(bf16[4,128,1280]{2,1,0:T(8,128)(2,1)} %t_ref.3), channel_id=1, source_target_pairs={{0,64},{64,128},{128,192},{192,256},{256,320},{320,384},{384,448},... | collective-permute-start | bytes 3932168 | tf_op jit(solution)/shard_map/ppermute | solution.py:152
  4.2 36.7 %collective-permute-start.2 = (bf16[2,128,1280]{2,1,0:T(8,128)(2,1)}, bf16[2,128,1280]{2,1,0:T(8,128)(2,1)S(1)}, u32[]{:S(2)}, u32[]{:S(2)}) collective-permute-start(bf16[2,128,1280]{2,1,0:T(8,128)(2,1)} %q_ref.3), channel_id=1, source_target_pairs={{0,896},{64,960},{128,0},{192,64},{256,128},{320,192},{384,256},{4... | collective-permute-start | bytes 1966088 | tf_op jit(solution)/shard_map/ppermute | solution.py:152
  12.9 28.0 %collective-permute-start = (s32[2]{0:T(128)}, s32[2]{0:T(128)S(1)}, u32[]{:S(2)}, u32[]{:S(2)}) collective-permute-start(s32[2]{0:T(128)} %qlen_ref.3), channel_id=1, source_target_pairs={{0,896},{64,960},{128,0},{192,64},{256,128},{320,192},{384,256},{4... | collective-permute-start | bytes 32 | tf_op jit(solution)/shard_map/ppermute | solution.py:152
  16.7 24.2 %collective-permute-start.1 = (s32[4]{0:T(128)}, s32[4]{0:T(128)S(1)}, u32[]{:S(2)}, u32[]{:S(2)}) collective-permute-start(s32[4]{0:T(128)} %tlen_ref.3), channel_id=1, source_target_pairs={{0,64},{64,128},{128,192},{192,256},{256,320},{320,384},{384,448},... | collective-permute-start | bytes 56 | tf_op jit(solution)/shard_map/ppermute | solution.py:152
  19.4 1.3 %copy-start = (bf16[4,128,1280]{2,1,0:T(8,128)(2,1)S(1)}, bf16[4,128,1280]{2,1,0:T(8,128)(2,1)}, u32[]{:S(2)}) copy-start(bf16[4,128,1280]{2,1,0:T(8,128)(2,1)} %t_ref.3) | copy-start | bytes 3932164
  20.8 1.1 %copy-start.1 = (bf16[2,128,1280]{2,1,0:T(8,128)(2,1)S(1)}, bf16[2,128,1280]{2,1,0:T(8,128)(2,1)}, u32[]{:S(2)}) copy-start(bf16[2,128,1280]{2,1,0:T(8,128)(2,1)} %q_ref.3) | copy-start | bytes 1966084
  21.8 0.7 copy-start.2
  22.5 0.7 copy-start.3
  45.8 4.9 %collective-permute-start.4 = (f32[32,8,1280]{2,1,0:T(8,128)S(1)}, f32[32,8,1280]{2,1,0:T(8,128)S(1)}, u32[]{:S(2)}, u32[]{:S(2)}) collective-permute-start(f32[32,8,1280]{2,1,0:T(8,128)S(1)} %get-tuple-element.13), channel_id=1, source_target_pairs={{0,1},{1,0},{2,3},{3,2},{4,5},{5,4},{6,7},{7,6},{8,9},{9,8},{10,11... | collective-permute-start | bytes 3932168 | tf_op jit(solution)/shard_map/ppermute | solution.py:183
  95.0 9.3 %collective-permute-start.5 = (f32[8,1280]{1,0:T(8,128)S(1)}, f32[8,1280]{1,0:T(8,128)S(1)}, u32[]{:S(2)}, u32[]{:S(2)}) collective-permute-start(f32[8,1280]{1,0:T(8,128)S(1)} %get-tuple-element.16), channel_id=1, source_target_pairs={{0,128},{64,192},{128,256},{192,320},{256,384},{320,448},{384,512}... | collective-permute-start | bytes 122888 | tf_op jit(solution)/shard_map/ppermute | solution.py:152

commit v2 on v1

--- a/solution.py
+++ b/solution.py
@@ -1,3 +1,4 @@
+import functools
 import math
 
 import jax
@@ -11,12 +12,13 @@
 BLK = ("zl", "y")
 GRP = ("x", "zh", "core")
 STEPS = 3
+MARK = 256.0
 NX, NZ = 8, 4
 F32 = jnp.float32
 BF16 = jnp.bfloat16
 
 
-def soft_block(q_ref, t_ref, qlen_ref, tlen_ref, offset, sims):
+def soft_block(q_ref, t_ref, qlen_ref, tlen_ref, lane, sims, first=0):
     queries, length, width = q_ref.shape
     blocks = t_ref.shape[0]
     scale = 3.0 / math.sqrt(width)
@@ -30,17 +32,19 @@
         * scale
     )
     lanes = lax.broadcasted_iota(jnp.int32, (length, length), 1)
-    rows = lax.broadcasted_iota(jnp.int32, (length, length), 0)
     place_row = lax.broadcasted_iota(jnp.int32, sims.shape, 0)
     place_lane = lax.broadcasted_iota(jnp.int32, sims.shape, 1)
     stacked = []
     for q in range(queries):
-        row_ok = rows < qlen_ref[q]
-        row_on = lax.broadcasted_iota(jnp.int32, (length, 1), 0) < qlen_ref[q]
+        if qlen_ref is None:
+            row_on = q_ref[q, :, 0:128].astype(F32)[:, 0:1] < 0.5 * MARK
+        else:
+            row_on = lax.broadcasted_iota(jnp.int32, (length, 1), 0) < qlen_ref[q]
+        row_ok = jnp.broadcast_to(row_on, (length, length))
         pieces = []
         for m in range(blocks):
-            col_ok = lanes < tlen_ref[m]
-            col_on = lax.broadcasted_iota(jnp.int32, (1, length), 1) < tlen_ref[m]
+            col_ok = lanes < tlen_ref[first + m]
+            col_on = lax.broadcasted_iota(jnp.int32, (1, length), 1) < tlen_ref[first + m]
             s = scores[q * length : (q + 1) * length, m * length : (m + 1) * length]
             by_row = jnp.where(col_ok, s, -jnp.inf)
             row_exp = jnp.exp(by_row - jnp.max(by_row, axis=1, keepdims=True))
@@ -51,21 +55,27 @@
             weights = row_soft + col_soft - row_soft * col_soft
             over = jnp.sum(jnp.sum(weights * s, axis=0, keepdims=True), axis=1, keepdims=True)
             under = jnp.sum(jnp.sum(weights, axis=0, keepdims=True), axis=1, keepdims=True)
-            here = jnp.logical_and(place_row == q, place_lane == offset * blocks + m)
+            here = jnp.logical_and(place_row == q, place_lane == lane + m)
             sims = jnp.where(here, over / under, sims)
             pieces.append(row_soft.astype(BF16))
         stacked.append(jnp.concatenate(pieces, axis=1))
     return jnp.concatenate(stacked, axis=0), sims
 
 
-def ordered(align, core_ref):
-    total = align.shape[0]
-    p = lax.broadcasted_iota(jnp.int32, (total, total), 0)
-    i = lax.broadcasted_iota(jnp.int32, (total, total), 1)
+def owner_order(core_ref, total, rows):
+    p = lax.broadcasted_iota(jnp.int32, (total, rows), 0)
+    i = lax.broadcasted_iota(jnp.int32, (total, rows), 1)
     core = jnp.bitwise_xor(p >> 8, core_ref[0])
     source = ((p >> 1) & 3) * 128 + ((p >> 3) & 31) * 4 + core * 2 + (p & 1)
-    pick = jnp.where(i == source, 1.0, 0.0).astype(BF16)
-    return jnp.dot(pick, align, preferred_element_type=F32).astype(BF16)
+    return jnp.where(i == source, 1.0, 0.0).astype(BF16)
+
+
+def share(core_ref, first, second, t_ref):
+    align = jnp.concatenate([first, second], axis=0)
+    pick = owner_order(core_ref, align.shape[0], align.shape[0])
+    align = jnp.dot(pick, align, preferred_element_type=F32).astype(BF16)
+    block = t_ref[...].reshape(t_ref.shape[0] * t_ref.shape[1], t_ref.shape[2])
+    return jnp.dot(align, block, preferred_element_type=F32)
 
 
 def own_kernel(qlen_ref, tlen_ref, q_ref, t_ref, align_ref, sims_ref):
@@ -74,21 +84,38 @@
     sims_ref[...] = sims
 
 
-def rest_kernel(
-    core_ref, qlen_ref, qlen2_ref, tlen_ref, tlen1_ref, q_ref, q2_ref, t_ref, t1_ref, align_ref, sims_ref,
-    mine_ref, theirs_ref, sims01_ref, sims23_ref, every_ref,
-):
-    flat = (t_ref.shape[0] * t_ref.shape[1], t_ref.shape[2])
-    rows, columns = align_ref.shape
-    every_ref[:rows, :columns] = align_ref[...]
-    every_ref[rows:, :columns], sims = soft_block(q2_ref, t_ref, qlen2_ref, tlen_ref, 2, jnp.zeros(sims_ref.shape, F32))
-    every_ref[:rows, columns:], sims01_ref[...] = soft_block(q_ref, t1_ref, qlen_ref, tlen1_ref, 1, sims_ref[...])
-    every_ref[rows:, columns:], sims23_ref[...] = soft_block(q2_ref, t1_ref, qlen2_ref, tlen1_ref, 3, sims)
-    align = ordered(every_ref[...], core_ref)
-    partial = jnp.dot(align[:, :columns], t_ref[...].reshape(flat), preferred_element_type=F32)
-    partial += jnp.dot(align[:, columns:], t1_ref[...].reshape(flat), preferred_element_type=F32)
-    mine_ref[...] = partial[:rows].reshape(mine_ref.shape)
-    theirs_ref[...] = partial[rows:].reshape(theirs_ref.shape)
+def near_kernel(core_ref, tlen_ref, q2_ref, t_ref, align_ref, partial_ref, sims23_ref):
+    second, sims = soft_block(q2_ref, t_ref, None, tlen_ref, 8, jnp.zeros(sims23_ref.shape, F32))
+    partial_ref[...] = share(core_ref, align_ref[...], second, t_ref)
+    sims23_ref[...] = sims
+
+
+def far_step(first, core_ref, qlen_ref, tlen1_ref, q_ref, q2_ref, t1_ref, partial_ref, sims01_ref, sims23_ref):
+    align, sims01 = soft_block(q_ref, t1_ref, qlen_ref, tlen1_ref, 4 + first, sims01_ref[...], first)
+    second, sims23 = soft_block(q2_ref, t1_ref, None, tlen1_ref, 12 + first, sims23_ref[...], first)
+    return partial_ref[...] + share(core_ref, align, second, t1_ref), sims01, sims23
+
+
+def middle_kernel(*refs):
+    *ins, out_ref, out01_ref, out23_ref = refs
+    out_ref[...], out01_ref[...], out23_ref[...] = far_step(0, *ins)
+
+
+def last_kernel(first, *refs):
+    *ins, mine_ref, theirs_ref, out01_ref, out23_ref = refs
+    partial, out01_ref[...], out23_ref[...] = far_step(first, *ins)
+    half = partial.shape[0] // 2
+    mine_ref[...] = partial[:half].reshape(mine_ref.shape)
+    theirs_ref[...] = partial[half:].reshape(theirs_ref.shape)
+
+
+def final_kernel(scale, own_ref, message_ref, sims_ref, profile_ref, similarity_ref):
+    count, rows = profile_ref.shape[:2]
+    columns = similarity_ref.shape[1]
+    total = (own_ref[...] + message_ref[0 : count * rows, :]) * scale
+    for q in range(count):
+        profile_ref[q] = total[q * rows : (q + 1) * rows]
+    similarity_ref[...] = sims_ref[0:count, 0:columns] + message_ref[count * rows : count * rows + count, 0:columns]
 
 
 def pack_kernel(mine_ref, theirs_ref, packed_ref, total_ref):
@@ -160,24 +187,33 @@
     struct = jax.ShapeDtypeStruct
     pair_flops = 2 * count * blocks * length * length * width
 
-    targets1 = moved_by(targets, 1)
-    queries2 = moved_by(queries, -2)
+    targets1 = [moved_by(targets, 1)]
+    spot = lax.broadcasted_iota(jnp.int32, (1, length, width), 1) >= query_lengths[core[0]]
+    spot = jnp.logical_and(spot, lax.broadcasted_iota(jnp.int32, (1, length, width), 2) == 0)
+    mine2 = jnp.where(spot, jnp.asarray(MARK, BF16), lax.dynamic_slice_in_dim(queries, core[0], 1))
+    mine2 = moved_by(mine2, -2)
     lengths1 = moved_by(target_lengths, 1)
-    query_lengths2 = moved_by(query_lengths, -2)
 
     sims_shape = struct((8, 128), F32)
     rows = count * length
-    align, sims = call(
+    align, sims01 = call(
         own_kernel, [query_lengths, target_lengths], [queries, targets],
         [struct((rows, blocks * length), BF16), sims_shape], pair_flops, "own_pairs",
     )
+    mine2, align = lax.optimization_barrier((mine2, align))
+    other2 = lax.ppermute(mine2, "core", [(0, 1), (1, 0)])
+    queries2 = jnp.where(core[0] == 0, jnp.concatenate([mine2, other2]), jnp.concatenate([other2, mine2]))
+    partial_shape = struct((2 * rows, width), F32)
+    partial, sims23 = call(
+        near_kernel, [core, target_lengths], [queries2, targets, align],
+        [partial_shape, sims_shape], 3 * pair_flops, "near_pairs",
+    )
+    scalars = [core, query_lengths, lengths1]
     owned = rows // (NX * NZ)
     halves = struct((NX * NZ, owned, width), F32)
     mine, theirs, sims01, sims23 = call(
-        rest_kernel, [core, query_lengths, query_lengths2, target_lengths, lengths1],
-        [queries, queries2, targets, targets1, align, sims],
-        [halves, halves, sims_shape, sims_shape], 8 * pair_flops, "other_pairs",
-        [pltpu.VMEM((2 * rows, 2 * blocks * length), BF16)],
+        functools.partial(last_kernel, 0), scalars, [queries, queries2, targets1[-1], partial, sims01, sims23],
+        [halves, halves, sims_shape, sims_shape], 4 * pair_flops, "last_pairs",
     )
 
     theirs = lax.ppermute(theirs, "core", [(0, 1), (1, 0)])
@@ -190,10 +226,11 @@
     packed = lax.all_to_all(packed.astype(jnp.float16), ("x", "zh"), 0, 0, tiled=True).astype(F32)
     own, message = call(packed_tail_kernel, [], [packed, sims23], ends, packed.size, "tail")
     message = moved_by(message, 2)
-    profile = (own + message[:half]) * profile_scale
-    columns = blocks * (STEPS + 1)
-    similarity = sims01[:count, :columns] + message[half : half + count, :columns]
-    return (profile.reshape(count, half // count, width), similarity)
+    profile, similarity = call(
+        functools.partial(final_kernel, profile_scale), [], [own, message, sims01],
+        [struct((count, half // count, width), F32), struct((count, blocks * (STEPS + 1)), F32)], own.size, "final",
+    )
+    return (profile, similarity)
 
 
 def solution(mesh):

time: 106 us -> 102 us (0.962)
  waiting for transfers between devices: 25.4 us -> 19.1 us
  Pallas kernels: 6.98 us -> 9.27 us
  starting transfers between devices: 23.9 us -> 22.1 us
  other arithmetic: 0.75 us -> 2.08 us
    ppermute x5 -> x4, waiting for transfers between devices: 22.4 us -> 16.1 us  [moved_by(): lax.ppermute(array, BLK, [(i, (i + by) % length) for i in range(length)])]
    ppermute x5 -> x4, starting transfers between devices: 21.9 us -> 18.3 us  [moved_by(): lax.ppermute(array, BLK, [(i, (i + by) % length) for i in range(length)])]
    pallas_call x4 -> x6, Pallas kernels: 6.98 us -> 9.27 us  [call(): pl.pallas_call(kernel, out_shape=outs, in_specs=[SMEM] * len(scalars) + [...]
    ppermute x0 -> x1, starting transfers between devices: none -> 1.91 us  [shards(): other2 = lax.ppermute(mine2, 'core', [(0, 1), (1, 0)])]
    select_n x0 -> x2, other arithmetic: none -> 1.25 us  [the longest x1 1.15 us: shards(): jnp.where(spot, jnp.asarray(MARK, BF16), lax.dynamic_slice_in_dim(queries...]
    dynamic_slice x0 -> x1, local copies, waits for them, and re-layouts: none -> 1.24 us  [shards(): query_lengths[core[0]]]
    unnamed x8 -> x12, local copies, waits for them, and re-layouts: 3.71 us -> 3.07 us
  transfers between devices with their start and end apart: 6 -> 6, of which waited for: 3 -> 4; matrix products, arithmetic and copies ran while one was open for 0% -> 3% of each run, Pallas kernels for 2% -> 5%
where the time goes in v2:
time: 102 us; the launch traced here: 101 us
  blocking collectives  43.4 us (43%)
  starting transfers between devices  22.1 us (22%)
  waiting for transfers between devices  19.1 us (19%)
  Pallas kernels  9.27 us (9%)
  local copies, waits for them, and re-layouts  4.31 us (4%)
  other arithmetic  2.08 us (2%)
    all_to_all x1, blocking collectives, shards(): lax.all_to_all(packed.astype(jnp.float16), ('x', 'zh'), 0, 0, tiled=True)  43.4 us
    ppermute x4, starting transfers between devices, moved_by(): lax.ppermute(array, BLK, [(i, (i + by) % length) for i in range(length)])  18.3 us
    ppermute x4, waiting for transfers between devices, moved_by(): lax.ppermute(array, BLK, [(i, (i + by) % length) for i in range(length)])  16.1 us
    pallas_call x6, Pallas kernels, call(): pl.pallas_call(kernel, out_shape=outs, in_specs=[SMEM] * len(scalars) + [...  9.27 us
    unnamed x12, local copies, waits for them, and re-layouts  3.07 us
    ppermute x1, waiting for transfers between devices, shards(): theirs = lax.ppermute(theirs, 'core', [(0, 1), (1, 0)])  3 us
  transfers between devices with their start and end apart: 6, of which 4 were waited for; matrix products, arithmetic and copies ran while one was open for 3% of the time, Pallas kernels for 5%

profile of v2, /device:TPU:2, one launch (start us, length us, event | category | flops | bytes accessed | tf_op | source)
XLA Modules:
  0.0 101.2 jit_solution(7597386856285751133)
XLA Ops:
  0.6 3.6 %collective-permute-start.3 = (bf16[4,128,1280]{2,1,0:T(8,128)(2,1)}, bf16[4,128,1280]{2,1,0:T(8,128)(2,1)S(1)}, u32[]{:S(2)}, u32[]{:S(2)}) collective-permute-start(bf16[4,128,1280]{2,1,0:T(8,128)(2,1)} %t_ref.3), channel_id=1, source_target_pairs={{0,64},{64,128},{128,192},{192,256},{256,320},{320,384},{384,448},... | collective-permute-start | bytes 3932168 | tf_op jit(solution)/shard_map/ppermute | solution.py:179
  4.3 1.2 %dynamic_slice.6 = s32[1]{0:T(128)} dynamic-slice(s32[2]{0:T(128)} %refs_1_.1, s32[]{:T(128)S(6)} %select_n.17), dynamic_slice_sizes={1} | dynamic-slice | bytes 12 | tf_op jit(solution)/shard_map/dynamic_slice | solution.py:191
  5.5 0.6 iota_compare_fusion.1
  6.2 1.1 %and_select_fusion = bf16[1,128,1280]{2,1,0:T(8,128)(2,1)S(1)} fusion(bf16[2,128,1280]{2,1,0:T(8,128)(2,1)} %refs_3_.1, s32[]{:T(128)S(6)} %select_n.17, pred[1280]{0:T(1024)(128)(4,1)S(1)} %iota_compare_fusion, pred[128]{0:T(512)(128)(4,1)S(1)} %iota_compare_fusion.1), kind=kLoop, calls=%fused_computation.1 | loop fusion | flops 327680 | bytes 656772 | tf_op jit(solution)/shard_map/jit(_where)/select_n | solution.py:193
  7.3 8.7 %collective-permute-start.1 = (bf16[1,128,1280]{2,1,0:T(8,128)(2,1)S(1)}, bf16[1,128,1280]{2,1,0:T(8,128)(2,1)S(1)}, u32[]{:S(2)}, u32[]{:S(2)}) collective-permute-start(bf16[1,128,1280]{2,1,0:T(8,128)(2,1)S(1)} %and_select_fusion), channel_id=1, source_target_pairs={{0,896},{64,960},{128,0},{192,64},{256,128},{320,192},{384,256},{4... | collective-permute-start | bytes 983048 | tf_op jit(solution)/shard_map/ppermute | solution.py:179
  16.0 1.1 %copy-done = bf16[2,128,1280]{2,1,0:T(8,128)(2,1)S(1)} copy-done((bf16[2,128,1280]{2,1,0:T(8,128)(2,1)S(1)}, bf16[2,128,1280]{2,1,0:T(8,128)(2,1)}, u32[]{:S(2)}) %copy-start) | copy-done | bytes 655384
  17.1 1.3 %copy-done.2 = bf16[4,128,1280]{2,1,0:T(8,128)(2,1)S(1)} copy-done((bf16[4,128,1280]{2,1,0:T(8,128)(2,1)S(1)}, bf16[4,128,1280]{2,1,0:T(8,128)(2,1)}, u32[]{:S(2)}) %copy-start.2) | copy-done | bytes 1310744
  18.4 0.7 copy-done.4
  19.0 1.9 %own_pairs.1 = (bf16[256,512]{1,0:T(8,128)(2,1)S(1)}, f32[8,128]{1,0:T(8,128)S(1)}) custom-call(s32[2]{0:T(128)S(1)} %copy-done.4, s32[4]{0:T(128)} %tlen_ref.3, bf16[2,128,1280]{2,1,0:T(8,128)(2,1)S(1)} %copy-done, bf16[4,128,1280]{2,1,0:T(8,128)(2,1)S(1)} %copy-done.2), custom_call_target="tpu_custom_call" | custom-call | flops 335544320 | bytes 2232320 | tf_op jit(solution)/shard_map/own_pairs/pallas_call | solution.py:165
  20.9 8.7 %collective-permute-done.1 = bf16[1,128,1280]{2,1,0:T(8,128)(2,1)S(1)} collective-permute-done((bf16[1,128,1280]{2,1,0:T(8,128)(2,1)S(1)}, bf16[1,128,1280]{2,1,0:T(8,128)(2,1)S(1)}, u32[]{:S(2)}, u32[]{:S(2)}) %collective-permute-start.1) | collective-permute-done | bytes 327712 | tf_op jit(solution)/shard_map/ppermute | solution.py:179
  29.6 1.9 %collective-permute-start.2 = (bf16[1,128,1280]{2,1,0:T(8,128)(2,1)S(1)}, bf16[1,128,1280]{2,1,0:T(8,128)(2,1)S(1)}, u32[]{:S(2)}, u32[]{:S(2)}) collective-permute-start(bf16[1,128,1280]{2,1,0:T(8,128)(2,1)S(1)} %collective-permute-done.1), channel_id=1, source_target_pairs={{0,1},{1,0},{2,3},{3,2},{4,5},{5,4},{6,7},{7,6},{8,9},{9,8},{10,11... | collective-permute-start | bytes 983048 | tf_op jit(solution)/shard_map/ppermute | solution.py:204
  31.6 1.9 %collective-permute-start = (s32[4]{0:T(128)}, s32[4]{0:T(128)S(1)}, u32[]{:S(2)}, u32[]{:S(2)}) collective-permute-start(s32[4]{0:T(128)} %tlen_ref.3), channel_id=1, source_target_pairs={{0,64},{64,128},{128,192},{192,256},{256,320},{320,384},{384,448},... | collective-permute-start | bytes 56 | tf_op jit(solution)/shard_map/ppermute | solution.py:179
  33.5 0.1 maximum_select_fusion.q2_ref.refs_4_
  33.7 3.0 %near_pairs.1 = (f32[512,1280]{1,0:T(8,128)S(1)}, f32[8,128]{1,0:T(8,128)S(1)}) custom-call(s32[1]{0:T(128)} %bitcast.core_ref.refs_0_, s32[4]{0:T(128)} %tlen_ref.3, bf16[2,128,1280]{2,1,0:T(8,128)(2,1)S(1)} %maximum_select_fusion.q2_ref.refs_4_, bf16[4,128,1280]{2,1,0:T(8,128)(2,1)S(1)} %copy-done.3, bf16[256,512]{1,0:T(8,128)(2,1)S(1)} %get-tuple-element.16.align_ref), custom_call_target="tpu_custom_call" | custom-call | flops 1006632960 | bytes 4853760 | tf_op jit(solution)/shard_map/near_pairs/pallas_call | solution.py:165
  36.7 2.6 %collective-permute-done.refs_2_ = s32[4]{0:T(128)S(1)} collective-permute-done((s32[4]{0:T(128)}, s32[4]{0:T(128)S(1)}, u32[]{:S(2)}, u32[]{:S(2)}) %collective-permute-start) | collective-permute-done | bytes 48 | tf_op jit(solution)/shard_map/ppermute | solution.py:179
  39.3 3.3 %last_pairs.1 = (f32[32,8,1280]{2,1,0:T(8,128)S(1)}, f32[32,8,1280]{2,1,0:T(8,128)S(1)}, f32[8,128]{1,0:T(8,128)S(1)}, f32[8,128]{1,0:T(8,128)S(1)}) custom-call(s32[1]{0:T(128)} %bitcast.core_ref.refs_0_, s32[2]{0:T(128)S(1)} %copy-done.5, s32[4]{0:T(128)S(1)} %collective-permute-done.refs_2_, bf16[2,128,1280]{2,1,0:T(8,128)(2,1)S(1)} %copy-done.1, ...), custom_call_target="tpu_custom_call" | custom-call | flops 1342177280 | bytes 7880704 | tf_op jit(solution)/shard_map/last_pairs/pallas_call | solution.py:165
  42.6 1.9 %collective-permute-start.4 = (f32[32,8,1280]{2,1,0:T(8,128)S(1)}, f32[32,8,1280]{2,1,0:T(8,128)S(1)}, u32[]{:S(2)}, u32[]{:S(2)}) collective-permute-start(f32[32,8,1280]{2,1,0:T(8,128)S(1)} %get-tuple-element.21), channel_id=1, source_target_pairs={{0,1},{1,0},{2,3},{3,2},{4,5},{5,4},{6,7},{7,6},{8,9},{9,8},{10,11... | collective-permute-start | bytes 3932168 | tf_op jit(solution)/shard_map/ppermute | solution.py:219
  44.5 3.0 %collective-permute-done.4.theirs_ref = f32[32,8,1280]{2,1,0:T(8,128)S(1)} collective-permute-done((f32[32,8,1280]{2,1,0:T(8,128)S(1)}, f32[32,8,1280]{2,1,0:T(8,128)S(1)}, u32[]{:S(2)}, u32[]{:S(2)}) %collective-permute-start.4) | collective-permute-done | bytes 1310752 | tf_op jit(solution)/shard_map/ppermute | solution.py:219
  47.5 0.3 pack.1
  47.9 43.4 %all_to_all.5 = f16[32,8,1408]{2,1,0:T(8,128)(2,1)S(1)} all-to-all(f16[32,8,1408]{2,1,0:T(8,128)(2,1)S(1)} %convert_element_type.6), channel_id=1, replica_groups=mesh['zl'=2,'y'=8,'x'=8,'zh'=4,'core'=2] {'x','zh'}, dimensions={0} | all-to-all | bytes 1441792 | tf_op jit(solution)/shard_map/all_to_all | solution.py:226
  91.5 0.2 tail.1
  91.6 4.1 %collective-permute-start.5 = (f32[8,1280]{1,0:T(8,128)S(1)}, f32[8,1280]{1,0:T(8,128)S(1)}, u32[]{:S(2)}, u32[]{:S(2)}) collective-permute-start(f32[8,1280]{1,0:T(8,128)S(1)} %get-tuple-element.24), channel_id=1, source_target_pairs={{0,128},{64,192},{128,256},{192,320},{256,384},{320,448},{384,512}... | collective-permute-start | bytes 122888 | tf_op jit(solution)/shard_map/ppermute | solution.py:179
  95.8 4.8 %collective-permute-done.5.message_ref = f32[8,1280]{1,0:T(8,128)S(1)} collective-permute-done((f32[8,1280]{1,0:T(8,128)S(1)}, f32[8,1280]{1,0:T(8,128)S(1)}, u32[]{:S(2)}, u32[]{:S(2)}) %collective-permute-start.5) | collective-permute-done | bytes 40992 | tf_op jit(solution)/shard_map/ppermute | solution.py:179
  100.5 0.6 final.1
  (14 shorter events, 0.2 us)
Async XLA Ops:
  0.6 38.6 %collective-permute-start.3 = (bf16[4,128,1280]{2,1,0:T(8,128)(2,1)}, bf16[4,128,1280]{2,1,0:T(8,128)(2,1)S(1)}, u32[]{:S(2)}, u32[]{:S(2)}) collective-permute-start(bf16[4,128,1280]{2,1,0:T(8,128)(2,1)} %t_ref.3), channel_id=1, source_target_pairs={{0,64},{64,128},{128,192},{192,256},{256,320},{320,384},{384,448},... | collective-permute-start | bytes 3932168 | tf_op jit(solution)/shard_map/ppermute | solution.py:179
  7.3 22.3 %collective-permute-start.1 = (bf16[1,128,1280]{2,1,0:T(8,128)(2,1)S(1)}, bf16[1,128,1280]{2,1,0:T(8,128)(2,1)S(1)}, u32[]{:S(2)}, u32[]{:S(2)}) collective-permute-start(bf16[1,128,1280]{2,1,0:T(8,128)(2,1)S(1)} %and_select_fusion), channel_id=1, source_target_pairs={{0,896},{64,960},{128,0},{192,64},{256,128},{320,192},{384,256},{4... | collective-permute-start | bytes 983048 | tf_op jit(solution)/shard_map/ppermute | solution.py:179
  16.0 1.1 %copy-start = (bf16[2,128,1280]{2,1,0:T(8,128)(2,1)S(1)}, bf16[2,128,1280]{2,1,0:T(8,128)(2,1)}, u32[]{:S(2)}) copy-start(bf16[2,128,1280]{2,1,0:T(8,128)(2,1)} %refs_3_.1) | copy-start | bytes 1966084
  17.1 1.3 %copy-start.2 = (bf16[4,128,1280]{2,1,0:T(8,128)(2,1)S(1)}, bf16[4,128,1280]{2,1,0:T(8,128)(2,1)}, u32[]{:S(2)}) copy-start(bf16[4,128,1280]{2,1,0:T(8,128)(2,1)} %t_ref.3) | copy-start | bytes 3932164
  18.4 0.7 copy-start.4
  19.0 14.6 %copy-start.3 = (bf16[4,128,1280]{2,1,0:T(8,128)(2,1)S(1)}, bf16[4,128,1280]{2,1,0:T(8,128)(2,1)}, u32[]{:S(2)}) copy-start(bf16[4,128,1280]{2,1,0:T(8,128)(2,1)} %t_ref.3) | copy-start | bytes 3932164
  29.6 3.9 %collective-permute-start.2 = (bf16[1,128,1280]{2,1,0:T(8,128)(2,1)S(1)}, bf16[1,128,1280]{2,1,0:T(8,128)(2,1)S(1)}, u32[]{:S(2)}, u32[]{:S(2)}) collective-permute-start(bf16[1,128,1280]{2,1,0:T(8,128)(2,1)S(1)} %collective-permute-done.1), channel_id=1, source_target_pairs={{0,1},{1,0},{2,3},{3,2},{4,5},{5,4},{6,7},{7,6},{8,9},{9,8},{10,11... | collective-permute-start | bytes 983048 | tf_op jit(solution)/shard_map/ppermute | solution.py:204
  31.6 7.7 %collective-permute-start = (s32[4]{0:T(128)}, s32[4]{0:T(128)S(1)}, u32[]{:S(2)}, u32[]{:S(2)}) collective-permute-start(s32[4]{0:T(128)} %tlen_ref.3), channel_id=1, source_target_pairs={{0,64},{64,128},{128,192},{192,256},{256,320},{320,384},{384,448},... | collective-permute-start | bytes 56 | tf_op jit(solution)/shard_map/ppermute | solution.py:179
  33.6 5.6 %copy-start.1 = (bf16[2,128,1280]{2,1,0:T(8,128)(2,1)S(1)}, bf16[2,128,1280]{2,1,0:T(8,128)(2,1)}, u32[]{:S(2)}) copy-start(bf16[2,128,1280]{2,1,0:T(8,128)(2,1)} %refs_3_.1) | copy-start | bytes 1966084
  33.6 5.6 %copy-start.5 = (s32[2]{0:T(128)S(1)}, s32[2]{0:T(128)}, u32[]{:S(2)}) copy-start(s32[2]{0:T(128)} %refs_1_.1) | copy-start | bytes 28
  42.6 4.9 %collective-permute-start.4 = (f32[32,8,1280]{2,1,0:T(8,128)S(1)}, f32[32,8,1280]{2,1,0:T(8,128)S(1)}, u32[]{:S(2)}, u32[]{:S(2)}) collective-permute-start(f32[32,8,1280]{2,1,0:T(8,128)S(1)} %get-tuple-element.21), channel_id=1, source_target_pairs={{0,1},{1,0},{2,3},{3,2},{4,5},{5,4},{6,7},{7,6},{8,9},{9,8},{10,11... | collective-permute-start | bytes 3932168 | tf_op jit(solution)/shard_map/ppermute | solution.py:219
  91.6 8.9 %collective-permute-start.5 = (f32[8,1280]{1,0:T(8,128)S(1)}, f32[8,1280]{1,0:T(8,128)S(1)}, u32[]{:S(2)}, u32[]{:S(2)}) collective-permute-start(f32[8,1280]{1,0:T(8,128)S(1)} %get-tuple-element.24), channel_id=1, source_target_pairs={{0,128},{64,192},{128,256},{192,320},{256,384},{320,448},{384,512}... | collective-permute-start | bytes 122888 | tf_op jit(solution)/shard_map/ppermute | solution.py:179

commit v3 on v2

--- a/solution.py
+++ b/solution.py
@@ -18,7 +18,7 @@
 BF16 = jnp.bfloat16
 
 
-def soft_block(q_ref, t_ref, qlen_ref, tlen_ref, lane, sims, first=0):
+def soft_block(q_ref, t_ref, qlen_ref, tlen_ref, lane, sims):
     queries, length, width = q_ref.shape
     blocks = t_ref.shape[0]
     scale = 3.0 / math.sqrt(width)
@@ -43,8 +43,8 @@
         row_ok = jnp.broadcast_to(row_on, (length, length))
         pieces = []
         for m in range(blocks):
-            col_ok = lanes < tlen_ref[first + m]
-            col_on = lax.broadcasted_iota(jnp.int32, (1, length), 1) < tlen_ref[first + m]
+            col_ok = lanes < tlen_ref[m]
+            col_on = lax.broadcasted_iota(jnp.int32, (1, length), 1) < tlen_ref[m]
             s = scores[q * length : (q + 1) * length, m * length : (m + 1) * length]
             by_row = jnp.where(col_ok, s, -jnp.inf)
             row_exp = jnp.exp(by_row - jnp.max(by_row, axis=1, keepdims=True))
@@ -70,12 +70,23 @@
     return jnp.where(i == source, 1.0, 0.0).astype(BF16)
 
 
-def share(core_ref, first, second, t_ref):
+def in_owner_order(core_ref, first, second):
     align = jnp.concatenate([first, second], axis=0)
     pick = owner_order(core_ref, align.shape[0], align.shape[0])
-    align = jnp.dot(pick, align, preferred_element_type=F32).astype(BF16)
+    return jnp.dot(pick, align, preferred_element_type=F32).astype(BF16)
+
+
+def profile_of(align, t_ref):
     block = t_ref[...].reshape(t_ref.shape[0] * t_ref.shape[1], t_ref.shape[2])
     return jnp.dot(align, block, preferred_element_type=F32)
+
+
+def fetch_kernel(core_ref, qlen_ref, q_ref, out_ref):
+    shape = (out_ref.shape[1], 128)
+    padding = lax.broadcasted_iota(jnp.int32, shape, 0) >= qlen_ref[core_ref[0]]
+    spot = jnp.logical_and(padding, lax.broadcasted_iota(jnp.int32, shape, 1) == 0)
+    out_ref[0] = q_ref[core_ref[0]]
+    out_ref[0, :, 0:128] = jnp.where(spot, MARK, q_ref[core_ref[0], :, 0:128].astype(F32)).astype(BF16)
 
 
 def own_kernel(qlen_ref, tlen_ref, q_ref, t_ref, align_ref, sims_ref):
@@ -84,29 +95,29 @@
     sims_ref[...] = sims
 
 
-def near_kernel(core_ref, tlen_ref, q2_ref, t_ref, align_ref, partial_ref, sims23_ref):
+def near_kernel(core_ref, tlen_ref, q2_ref, t_ref, align_ref, mine_ref, theirs_ref, sims23_ref):
     second, sims = soft_block(q2_ref, t_ref, None, tlen_ref, 8, jnp.zeros(sims23_ref.shape, F32))
-    partial_ref[...] = share(core_ref, align_ref[...], second, t_ref)
+    partial = profile_of(in_owner_order(core_ref, align_ref[...], second), t_ref)
+    half = partial.shape[0] // 2
+    mine_ref[...] = partial[:half]
+    theirs_ref[...] = partial[half:]
     sims23_ref[...] = sims
 
 
-def far_step(first, core_ref, qlen_ref, tlen1_ref, q_ref, q2_ref, t1_ref, partial_ref, sims01_ref, sims23_ref):
-    align, sims01 = soft_block(q_ref, t1_ref, qlen_ref, tlen1_ref, 4 + first, sims01_ref[...], first)
-    second, sims23 = soft_block(q2_ref, t1_ref, None, tlen1_ref, 12 + first, sims23_ref[...], first)
-    return partial_ref[...] + share(core_ref, align, second, t1_ref), sims01, sims23
-
-
-def middle_kernel(*refs):
-    *ins, out_ref, out01_ref, out23_ref = refs
-    out_ref[...], out01_ref[...], out23_ref[...] = far_step(0, *ins)
-
-
-def last_kernel(first, *refs):
-    *ins, mine_ref, theirs_ref, out01_ref, out23_ref = refs
-    partial, out01_ref[...], out23_ref[...] = far_step(first, *ins)
-    half = partial.shape[0] // 2
-    mine_ref[...] = partial[:half].reshape(mine_ref.shape)
-    theirs_ref[...] = partial[half:].reshape(theirs_ref.shape)
+def far_kernel(
+    core_ref, qlen_ref, tlen1_ref, q_ref, q2_ref, t1_ref, near_ref, sims01_ref, sims23_ref,
+    theirs_ref, align_ref, out01_ref, out23_ref,
+):
+    first, out01_ref[...] = soft_block(q_ref, t1_ref, qlen_ref, tlen1_ref, 4, sims01_ref[...])
+    second, out23_ref[...] = soft_block(q2_ref, t1_ref, None, tlen1_ref, 12, sims23_ref[...])
+    align = in_owner_order(core_ref, first, second)
+    half = align.shape[0] // 2
+    theirs_ref[...] = (near_ref[...] + profile_of(align[half:], t1_ref)).reshape(theirs_ref.shape)
+    align_ref[...] = align[:half]
+
+
+def mine_kernel(align_ref, t1_ref, near_ref, mine_ref):
+    mine_ref[...] = (near_ref[...] + profile_of(align_ref[...], t1_ref)).reshape(mine_ref.shape)
 
 
 def final_kernel(scale, own_ref, message_ref, sims_ref, profile_ref, similarity_ref):
@@ -187,10 +198,10 @@
     struct = jax.ShapeDtypeStruct
     pair_flops = 2 * count * blocks * length * length * width
 
-    targets1 = [moved_by(targets, 1)]
-    spot = lax.broadcasted_iota(jnp.int32, (1, length, width), 1) >= query_lengths[core[0]]
-    spot = jnp.logical_and(spot, lax.broadcasted_iota(jnp.int32, (1, length, width), 2) == 0)
-    mine2 = jnp.where(spot, jnp.asarray(MARK, BF16), lax.dynamic_slice_in_dim(queries, core[0], 1))
+    targets1 = moved_by(targets, 1)
+    (mine2,) = call(
+        fetch_kernel, [core, query_lengths], [queries], [struct((1, length, width), BF16)], queries.size, "fetch"
+    )
     mine2 = moved_by(mine2, -2)
     lengths1 = moved_by(target_lengths, 1)
 
@@ -203,20 +214,20 @@
     mine2, align = lax.optimization_barrier((mine2, align))
     other2 = lax.ppermute(mine2, "core", [(0, 1), (1, 0)])
     queries2 = jnp.where(core[0] == 0, jnp.concatenate([mine2, other2]), jnp.concatenate([other2, mine2]))
-    partial_shape = struct((2 * rows, width), F32)
-    partial, sims23 = call(
+    partial_shape = struct((rows, width), F32)
+    near_mine, near_theirs, sims23 = call(
         near_kernel, [core, target_lengths], [queries2, targets, align],
-        [partial_shape, sims_shape], 3 * pair_flops, "near_pairs",
-    )
-    scalars = [core, query_lengths, lengths1]
+        [partial_shape, partial_shape, sims_shape], 3 * pair_flops, "near_pairs",
+    )
     owned = rows // (NX * NZ)
     halves = struct((NX * NZ, owned, width), F32)
-    mine, theirs, sims01, sims23 = call(
-        functools.partial(last_kernel, 0), scalars, [queries, queries2, targets1[-1], partial, sims01, sims23],
-        [halves, halves, sims_shape, sims_shape], 4 * pair_flops, "last_pairs",
+    theirs, align, sims01, sims23 = call(
+        far_kernel, [core, query_lengths, lengths1], [queries, queries2, targets1, near_theirs, sims01, sims23],
+        [halves, struct((rows, blocks * length), BF16), sims_shape, sims_shape], 3 * pair_flops, "far_pairs",
     )
 
     theirs = lax.ppermute(theirs, "core", [(0, 1), (1, 0)])
+    (mine,) = call(mine_kernel, [], [align, targets1, near_mine], [halves], pair_flops, "own_rows")
     packed_shape = struct((NX * NZ, owned, width + 128), F32)
     (packed,) = call(
         pack_kernel, [], [mine, theirs], [packed_shape], 8 * mine.size, "pack", [pltpu.VMEM(mine.shape, F32)]

time: 102 us -> 102 us (level)
  local copies, waits for them, and re-layouts: 4.31 us -> 3.06 us
  Pallas kernels: 9.27 us -> 10.3 us
    select_n x1, other arithmetic: 0.11 us -> 1.4 us  [shards(): jnp.where(core[0] == 0, jnp.concatenate([mine2, other2]), jnp.concatenate...]
    dynamic_slice x1 -> x0, local copies, waits for them, and re-layouts: 1.24 us -> none  [shards(): query_lengths[core[0]]]
    select_n x1 -> x0, other arithmetic: 1.15 us -> none  [shards(): jnp.where(spot, jnp.asarray(MARK, BF16), lax.dynamic_slice_in_dim(queries...]
    pallas_call x6 -> x8, Pallas kernels: 9.27 us -> 10.3 us  [call(): pl.pallas_call(kernel, out_shape=outs, in_specs=[SMEM] * len(scalars) + [...]
  transfers between devices with their start and end apart: 6 -> 6, of which waited for: 4 -> 4; matrix products, arithmetic and copies ran while one was open for 3% -> 1% of each run, Pallas kernels for 5% -> 6%
where the time goes in v3:
time: 102 us; the launch traced here: 101 us
  blocking collectives  43.9 us (43%)
  starting transfers between devices  22.9 us (22%)
  waiting for transfers between devices  18.8 us (18%)
  Pallas kernels  10.3 us (10%)
  local copies, waits for them, and re-layouts  3.06 us (3%)
  other arithmetic  1.57 us (2%)
    all_to_all x1, blocking collectives, shards(): lax.all_to_all(packed.astype(jnp.float16), ('x', 'zh'), 0, 0, tiled=True)  43.9 us
    ppermute x4, starting transfers between devices, moved_by(): lax.ppermute(array, BLK, [(i, (i + by) % length) for i in range(length)])  19.1 us
    ppermute x4, waiting for transfers between devices, moved_by(): lax.ppermute(array, BLK, [(i, (i + by) % length) for i in range(length)])  16.3 us
    pallas_call x8, Pallas kernels, call(): pl.pallas_call(kernel, out_shape=outs, in_specs=[SMEM] * len(scalars) + [...  10.3 us
    unnamed x12, local copies, waits for them, and re-layouts  3.06 us
    ppermute x1, waiting for transfers between devices, shards(): theirs = lax.ppermute(theirs, 'core', [(0, 1), (1, 0)])  2.49 us
  transfers between devices with their start and end apart: 6, of which 4 were waited for; matrix products, arithmetic and copies ran while one was open for 1% of the time, Pallas kernels for 6%

profile of v3, /device:TPU:2, one launch (start us, length us, event | category | flops | bytes accessed | tf_op | source)
XLA Modules:
  0.0 101.4 jit_solution(1285562007653483351)
XLA Ops:
  0.6 3.6 %collective-permute-start.3 = (bf16[4,128,1280]{2,1,0:T(8,128)(2,1)}, bf16[4,128,1280]{2,1,0:T(8,128)(2,1)S(1)}, u32[]{:S(2)}, u32[]{:S(2)}) collective-permute-start(bf16[4,128,1280]{2,1,0:T(8,128)(2,1)} %t_ref.3), channel_id=1, source_target_pairs={{0,64},{64,128},{128,192},{192,256},{256,320},{320,384},{384,448},... | collective-permute-start | bytes 3932168 | tf_op jit(solution)/shard_map/ppermute | solution.py:190
  4.3 1.1 %copy-done = bf16[2,128,1280]{2,1,0:T(8,128)(2,1)S(1)} copy-done((bf16[2,128,1280]{2,1,0:T(8,128)(2,1)S(1)}, bf16[2,128,1280]{2,1,0:T(8,128)(2,1)}, u32[]{:S(2)}) %copy-start) | copy-done | bytes 655384
  5.3 0.7 copy-done.4
  6.0 0.6 fetch.1
  6.6 8.7 %collective-permute-start.1 = (bf16[1,128,1280]{2,1,0:T(8,128)(2,1)S(1)}, bf16[1,128,1280]{2,1,0:T(8,128)(2,1)}, u32[]{:S(2)}, u32[]{:S(2)}) collective-permute-start(bf16[1,128,1280]{2,1,0:T(8,128)(2,1)S(1)} %fetch.1), channel_id=1, source_target_pairs={{0,896},{64,960},{128,0},{192,64},{256,128},{320,192},{384,256},{4... | collective-permute-start | bytes 983048 | tf_op jit(solution)/shard_map/ppermute | solution.py:190
  15.3 1.3 %copy-done.2 = bf16[4,128,1280]{2,1,0:T(8,128)(2,1)S(1)} copy-done((bf16[4,128,1280]{2,1,0:T(8,128)(2,1)S(1)}, bf16[4,128,1280]{2,1,0:T(8,128)(2,1)}, u32[]{:S(2)}) %copy-start.2) | copy-done | bytes 1310744
  16.6 1.9 %own_pairs.1 = (bf16[256,512]{1,0:T(8,128)(2,1)S(1)}, f32[8,128]{1,0:T(8,128)S(1)}) custom-call(s32[2]{0:T(128)S(1)} %copy-done.4, s32[4]{0:T(128)} %tlen_ref.3, bf16[2,128,1280]{2,1,0:T(8,128)(2,1)S(1)} %copy-done.1, bf16[4,128,1280]{2,1,0:T(8,128)(2,1)S(1)} %copy-done.2), custom_call_target="tpu_custom_call" | custom-call | flops 335544320 | bytes 2232320 | tf_op jit(solution)/shard_map/own_pairs/pallas_call | solution.py:176
  18.4 10.5 %collective-permute-done.1 = bf16[1,128,1280]{2,1,0:T(8,128)(2,1)} collective-permute-done((bf16[1,128,1280]{2,1,0:T(8,128)(2,1)S(1)}, bf16[1,128,1280]{2,1,0:T(8,128)(2,1)}, u32[]{:S(2)}, u32[]{:S(2)}) %collective-permute-start.1) | collective-permute-done | bytes 327712 | tf_op jit(solution)/shard_map/ppermute | solution.py:190
  28.9 1.9 %collective-permute-start.2 = (bf16[1,128,1280]{2,1,0:T(8,128)(2,1)}, bf16[1,128,1280]{2,1,0:T(8,128)(2,1)}, u32[]{:S(2)}, u32[]{:S(2)}) collective-permute-start(bf16[1,128,1280]{2,1,0:T(8,128)(2,1)} %collective-permute-done.1), channel_id=1, source_target_pairs={{0,1},{1,0},{2,3},{3,2},{4,5},{5,4},{6,7},{7,6},{8,9},{9,8},{10,11... | collective-permute-start | bytes 983048 | tf_op jit(solution)/shard_map/ppermute | solution.py:215
  30.8 1.9 %collective-permute-start = (s32[4]{0:T(128)}, s32[4]{0:T(128)S(1)}, u32[]{:S(2)}, u32[]{:S(2)}) collective-permute-start(s32[4]{0:T(128)} %tlen_ref.3), channel_id=1, source_target_pairs={{0,64},{64,128},{128,192},{192,256},{256,320},{320,384},{384,448},... | collective-permute-start | bytes 56 | tf_op jit(solution)/shard_map/ppermute | solution.py:190
  32.8 1.4 %maximum_select_fusion.q2_ref = bf16[2,128,1280]{2,1,0:T(8,128)(2,1)S(1)} fusion(bf16[1,128,1280]{2,1,0:T(8,128)(2,1)} %collective-permute-done.2, bf16[1,128,1280]{2,1,0:T(8,128)(2,1)} %collective-permute-done.1, pred[]{:T(512)S(6)} %eq.3), kind=kLoop, calls=%fused_computation | loop fusion | flops 983040 | bytes 1310721 | tf_op jit(solution)/shard_map/jit(_where)/select_n | solution.py:216
  34.2 3.0 %near_pairs.1 = (f32[256,1280]{1,0:T(8,128)S(1)}, f32[256,1280]{1,0:T(8,128)S(1)}, f32[8,128]{1,0:T(8,128)S(1)}) custom-call(s32[1]{0:T(128)} %bitcast.core_ref, s32[4]{0:T(128)} %tlen_ref.3, bf16[2,128,1280]{2,1,0:T(8,128)(2,1)S(1)} %maximum_select_fusion.q2_ref, bf16[4,128,1280]{2,1,0:T(8,128)(2,1)S(1)} %copy-done.3, ...), custom_call_target="tpu_custom_call" | custom-call | flops 1006632960 | bytes 4853760 | tf_op jit(solution)/shard_map/near_pairs/pallas_call | solution.py:176
  37.2 1.4 %collective-permute-done.tlen1_ref = s32[4]{0:T(128)S(1)} collective-permute-done((s32[4]{0:T(128)}, s32[4]{0:T(128)S(1)}, u32[]{:S(2)}, u32[]{:S(2)}) %collective-permute-start) | collective-permute-done | bytes 48 | tf_op jit(solution)/shard_map/ppermute | solution.py:190
  38.6 3.3 %far_pairs.1 = (f32[32,8,1280]{2,1,0:T(8,128)S(1)}, bf16[256,512]{1,0:T(8,128)(2,1)S(1)}, f32[8,128]{1,0:T(8,128)S(1)}, f32[8,128]{1,0:T(8,128)S(1)}) custom-call(s32[1]{0:T(128)} %bitcast.core_ref, s32[2]{0:T(128)S(1)} %copy-done.5, s32[4]{0:T(128)S(1)} %collective-permute-done.tlen1_ref, bf16[2,128,1280]{2,1,0:T(8,128)(2,1)S(1)} %copy-done.1, ...), custom_call_target="tpu_custom_call" | custom-call | flops 1006632960 | bytes 5521408 | tf_op jit(solution)/shard_map/far_pairs/pallas_call | solution.py:176
  41.9 1.9 %collective-permute-start.4 = (f32[32,8,1280]{2,1,0:T(8,128)S(1)}, f32[32,8,1280]{2,1,0:T(8,128)S(1)}, u32[]{:S(2)}, u32[]{:S(2)}) collective-permute-start(f32[32,8,1280]{2,1,0:T(8,128)S(1)} %get-tuple-element.23), channel_id=1, source_target_pairs={{0,1},{1,0},{2,3},{3,2},{4,5},{5,4},{6,7},{7,6},{8,9},{9,8},{10,11... | collective-permute-start | bytes 3932168 | tf_op jit(solution)/shard_map/ppermute | solution.py:229
  43.8 0.5 own_rows.1.mine_ref
  44.4 2.5 %collective-permute-done.4.theirs_ref = f32[32,8,1280]{2,1,0:T(8,128)S(1)} collective-permute-done((f32[32,8,1280]{2,1,0:T(8,128)S(1)}, f32[32,8,1280]{2,1,0:T(8,128)S(1)}, u32[]{:S(2)}, u32[]{:S(2)}) %collective-permute-start.4) | collective-permute-done | bytes 1310752 | tf_op jit(solution)/shard_map/ppermute | solution.py:229
  46.8 0.3 pack.1
  47.3 43.9 %all_to_all.5 = f16[32,8,1408]{2,1,0:T(8,128)(2,1)S(1)} all-to-all(f16[32,8,1408]{2,1,0:T(8,128)(2,1)S(1)} %convert_element_type.6), channel_id=1, replica_groups=mesh['zl'=2,'y'=8,'x'=8,'zh'=4,'core'=2] {'x','zh'}, dimensions={0} | all-to-all | bytes 1441792 | tf_op jit(solution)/shard_map/all_to_all | solution.py:237
  91.1 0.1 convert_element_type.7.packed_ref
  91.2 0.2 tail.1
  91.4 4.9 %collective-permute-start.5 = (f32[8,1280]{1,0:T(8,128)S(1)}, f32[8,1280]{1,0:T(8,128)S(1)}, u32[]{:S(2)}, u32[]{:S(2)}) collective-permute-start(f32[8,1280]{1,0:T(8,128)S(1)} %get-tuple-element.26), channel_id=1, source_target_pairs={{0,128},{64,192},{128,256},{192,320},{256,384},{320,448},{384,512}... | collective-permute-start | bytes 122888 | tf_op jit(solution)/shard_map/ppermute | solution.py:190
  96.3 4.4 %collective-permute-done.5.message_ref = f32[8,1280]{1,0:T(8,128)S(1)} collective-permute-done((f32[8,1280]{1,0:T(8,128)S(1)}, f32[8,1280]{1,0:T(8,128)S(1)}, u32[]{:S(2)}, u32[]{:S(2)}) %collective-permute-start.5) | collective-permute-done | bytes 40992 | tf_op jit(solution)/shard_map/ppermute | solution.py:190
  100.7 0.6 final.1
  (12 shorter events, 0.1 us)
Async XLA Ops:
  0.6 38.0 %collective-permute-start.3 = (bf16[4,128,1280]{2,1,0:T(8,128)(2,1)}, bf16[4,128,1280]{2,1,0:T(8,128)(2,1)S(1)}, u32[]{:S(2)}, u32[]{:S(2)}) collective-permute-start(bf16[4,128,1280]{2,1,0:T(8,128)(2,1)} %t_ref.3), channel_id=1, source_target_pairs={{0,64},{64,128},{128,192},{192,256},{256,320},{320,384},{384,448},... | collective-permute-start | bytes 3932168 | tf_op jit(solution)/shard_map/ppermute | solution.py:190
  4.2 1.1 %copy-start = (bf16[2,128,1280]{2,1,0:T(8,128)(2,1)S(1)}, bf16[2,128,1280]{2,1,0:T(8,128)(2,1)}, u32[]{:S(2)}) copy-start(bf16[2,128,1280]{2,1,0:T(8,128)(2,1)} %q_ref.5) | copy-start | bytes 1966084
  5.3 0.7 copy-start.4
  6.0 9.3 %copy-start.1 = (bf16[2,128,1280]{2,1,0:T(8,128)(2,1)S(1)}, bf16[2,128,1280]{2,1,0:T(8,128)(2,1)}, u32[]{:S(2)}) copy-start(bf16[2,128,1280]{2,1,0:T(8,128)(2,1)} %q_ref.5) | copy-start | bytes 1966084
  6.6 22.3 %collective-permute-start.1 = (bf16[1,128,1280]{2,1,0:T(8,128)(2,1)S(1)}, bf16[1,128,1280]{2,1,0:T(8,128)(2,1)}, u32[]{:S(2)}, u32[]{:S(2)}) collective-permute-start(bf16[1,128,1280]{2,1,0:T(8,128)(2,1)S(1)} %fetch.1), channel_id=1, source_target_pairs={{0,896},{64,960},{128,0},{192,64},{256,128},{320,192},{384,256},{4... | collective-permute-start | bytes 983048 | tf_op jit(solution)/shard_map/ppermute | solution.py:190
  15.3 1.3 %copy-start.2 = (bf16[4,128,1280]{2,1,0:T(8,128)(2,1)S(1)}, bf16[4,128,1280]{2,1,0:T(8,128)(2,1)}, u32[]{:S(2)}) copy-start(bf16[4,128,1280]{2,1,0:T(8,128)(2,1)} %t_ref.3) | copy-start | bytes 3932164
  16.6 17.6 %copy-start.3 = (bf16[4,128,1280]{2,1,0:T(8,128)(2,1)S(1)}, bf16[4,128,1280]{2,1,0:T(8,128)(2,1)}, u32[]{:S(2)}) copy-start(bf16[4,128,1280]{2,1,0:T(8,128)(2,1)} %t_ref.3) | copy-start | bytes 3932164
  28.9 3.9 %collective-permute-start.2 = (bf16[1,128,1280]{2,1,0:T(8,128)(2,1)}, bf16[1,128,1280]{2,1,0:T(8,128)(2,1)}, u32[]{:S(2)}, u32[]{:S(2)}) collective-permute-start(bf16[1,128,1280]{2,1,0:T(8,128)(2,1)} %collective-permute-done.1), channel_id=1, source_target_pairs={{0,1},{1,0},{2,3},{3,2},{4,5},{5,4},{6,7},{7,6},{8,9},{9,8},{10,11... | collective-permute-start | bytes 983048 | tf_op jit(solution)/shard_map/ppermute | solution.py:215
  30.8 7.8 %collective-permute-start = (s32[4]{0:T(128)}, s32[4]{0:T(128)S(1)}, u32[]{:S(2)}, u32[]{:S(2)}) collective-permute-start(s32[4]{0:T(128)} %tlen_ref.3), channel_id=1, source_target_pairs={{0,64},{64,128},{128,192},{192,256},{256,320},{320,384},{384,448},... | collective-permute-start | bytes 56 | tf_op jit(solution)/shard_map/ppermute | solution.py:190
  34.2 4.4 %copy-start.5 = (s32[2]{0:T(128)S(1)}, s32[2]{0:T(128)}, u32[]{:S(2)}) copy-start(s32[2]{0:T(128)} %qlen_ref.5) | copy-start | bytes 28
  41.9 4.9 %collective-permute-start.4 = (f32[32,8,1280]{2,1,0:T(8,128)S(1)}, f32[32,8,1280]{2,1,0:T(8,128)S(1)}, u32[]{:S(2)}, u32[]{:S(2)}) collective-permute-start(f32[32,8,1280]{2,1,0:T(8,128)S(1)} %get-tuple-element.23), channel_id=1, source_target_pairs={{0,1},{1,0},{2,3},{3,2},{4,5},{5,4},{6,7},{7,6},{8,9},{9,8},{10,11... | collective-permute-start | bytes 3932168 | tf_op jit(solution)/shard_map/ppermute | solution.py:229
  91.4 9.3 %collective-permute-start.5 = (f32[8,1280]{1,0:T(8,128)S(1)}, f32[8,1280]{1,0:T(8,128)S(1)}, u32[]{:S(2)}, u32[]{:S(2)}) collective-permute-start(f32[8,1280]{1,0:T(8,128)S(1)} %get-tuple-element.26), channel_id=1, source_target_pairs={{0,128},{64,192},{128,256},{192,320},{256,384},{320,448},{384,512}... | collective-permute-start | bytes 122888 | tf_op jit(solution)/shard_map/ppermute | solution.py:190
